TPU v7x, 256 devices: a whole 4x4x8 slice. The times are simulated.
256 devices in a mesh: row: 16 (over y, x), col: 16 (over z, core).
Axes of the slice: x: 4, y: 4, z: 8, core: 2. Of those that a mesh axis runs over, the one named last changes fastest.
Arguments:
- targets: float32 [2, 131072], P(None, ('row', 'col')), may hold values from 0 to 1
- sources: bfloat16 [2, 32768], P(None, 'col'), may hold values from 0 to 1
- omega: bfloat16 [256, 32768], P(None, 'col'), may hold values from -0.03125 to 0.03125
- tree_order: int32 [131072], P(('row', 'col')), may hold values from 0 to 131071, each once
- leaf_pivots: int32 [256, 128], P(('row', 'col')), may hold values from 0 to 511, all different within a row
- pivots_one: int32 [128, 128], replicated, may hold values from 0 to 255, all different within a row
- pivots_two: int32 [64, 128], replicated, may hold values from 0 to 255, all different within a row
- pivots_three: int32 [32, 128], replicated, may hold values from 0 to 255, all different within a row
Outputs:
- leaf_interp: float32 [131072, 128], P(('row', 'col'))
- level_one_interp: float32 [32768, 128], P(('row', 'col'))
- level_two_interp: float32 [16384, 128], P(('row', 'col'))
- level_three_interp: float32 [8192, 128], P(('row', 'col'))
- root_sketch: float32 [4096, 256], P(('row', 'col'))
Inputs may be any that keep to these rules, and one draw needn't show every extreme that they name: tree_order names every target point once. `leaf_pivots`: each row names 128 distinct positions. `pivots_one`: each row names 128 distinct positions. `pivots_two`: each row names 128 distinct positions. `pivots_three`: each row names 128 distinct positions.
All inputs are finite; a program needn't handle non-finite values.
Results may differ from a plain program's by a relative error of at most 0.0074.
Values may be sent and summed in bfloat16 or wider, within the bound.
No kernel may reach another device: no remote copies, remote signals or barrier semaphores. Data moves between devices by JAX's collectives and lax.ppermute only.
A program may use at most 192 MiB of HBM per device.

v0:
```python
import math
import jax
import jax.numpy as jnp
from jax import lax
from jax.sharding import Mesh
from jax.sharding import PartitionSpec as P

LEAF = 512
S = 256
LEVELS = 3
ROW_COL = ("row_0", "row_1", "col_0", "col_1")
COL = ("col_0", "col_1")
ROW = ("row_0", "row_1")
RIDGE = 0.1
DELTA_SQUARED = 0.0001


def copy_for_each(value, axis):
    copies = jnp.broadcast_to(value, (lax.axis_size(axis), *value.shape))
    return lax.all_to_all(copies, axis, split_axis=0, concat_axis=0, tiled=True)


def laid_out(parts, dim):
    parts = jnp.moveaxis(parts, 0, dim)
    shape = parts.shape
    return parts.reshape(*shape[:dim], shape[dim] * shape[dim + 1], *shape[dim + 2 :])


def gathered_by_axis(value, axes, dim):
    far, near = axes
    parts = copy_for_each(copy_for_each(value, far), near)
    return laid_out(parts.swapaxes(0, 1).reshape(-1, *value.shape), dim)


def partner_2(block, axis, stride):
    count = lax.axis_size(axis)
    route = []
    for low in range(count):
        high = low | 1 << stride
        if high != low and high < count:
            route += [(low, high), (high, low)]
    return lax.ppermute(block, axis, route)


def kernel_block(points, source_pts):
    delta_x = points[0][:, None] - source_pts[0][None, :].astype(jnp.float32)
    delta_y = points[1][:, None] - source_pts[1][None, :].astype(jnp.float32)
    return (-0.5 * jnp.log(delta_x * delta_x + delta_y * delta_y + DELTA_SQUARED)).astype(
        jnp.bfloat16
    )


def select_factor(candidates, pivots):
    chosen = jnp.take(candidates, pivots, axis=0)
    gram_matrix = jnp.dot(chosen, chosen.T, precision=lax.Precision.HIGHEST)
    ridge_shift = RIDGE * (jnp.trace(gram_matrix) / chosen.shape[0] + 1e-06)
    shifted = gram_matrix + ridge_shift * jnp.eye(chosen.shape[0], dtype=gram_matrix.dtype)
    return (chosen, jnp.linalg.cholesky(shifted))


def solve_rows(chosen, factor, row_block):
    right_side = jnp.dot(chosen, row_block.T, precision=lax.Precision.HIGHEST)
    first = lax.linalg.triangular_solve(factor, right_side, left_side=True, lower=True)
    second = lax.linalg.triangular_solve(
        factor, first, left_side=True, lower=True, transpose_a=True
    )
    return second.T


def sketch_product(points, source_pts, weights):
    panel = kernel_block(points, source_pts)
    return lax.dot_general(
        panel, weights, (((1,), (1,)), ((), ())), preferred_element_type=jnp.float32
    )


def body(targets, sources, omega, tree_order, leaf_pivots, pivots_one, pivots_two, pivots_three):
    everyone = gathered_by_axis(targets, ("row_0", ("row_1", "col_0", "col_1")), 1)
    col_count = lax.axis_size(COL)
    col_index = lax.axis_index(COL)
    row_index = lax.axis_index(ROW)
    global_index = row_index * col_count + col_index
    own_points = jnp.take(everyone, tree_order, axis=1)
    initial = jnp.zeros((LEAF, S), jnp.float32)
    running = initial
    pieces = (
        lax.all_gather(sources, COL, axis=1, tiled=True),
        lax.all_gather(omega, COL, axis=1, tiled=True),
    )
    width = pieces[0].shape[1]
    block_len = math.gcd(width, 1024)
    source_blocks = pieces[0].reshape(2, width // block_len, block_len).transpose(1, 0, 2)
    weight_blocks = pieces[1].reshape(S, width // block_len, block_len).transpose(1, 0, 2)

    def add_block(carried, items):
        return (carried + sketch_product(own_points, items[0], items[1]), None)

    running, unused = lax.scan(add_block, running, (source_blocks, weight_blocks))
    chosen, factor = select_factor(running, leaf_pivots[0])
    results = [solve_rows(chosen, factor, running)]
    tables = (pivots_one, pivots_two, pivots_three)
    for section in range(LEVELS):
        partner = partner_2(chosen, COL, section)
        high_half = col_index >> section & 1 == 1
        candidates = jnp.where(
            high_half, jnp.concatenate([partner, chosen], 0), jnp.concatenate([chosen, partner], 0)
        )
        node_index = global_index >> section + 1
        node_pivots = lax.dynamic_index_in_dim(tables[section], node_index, 0, keepdims=False)
        group_size = 2 ** (section + 1)
        share_rows = candidates.shape[0] // group_size
        my_rows = lax.dynamic_slice_in_dim(
            candidates, col_index % group_size * share_rows, share_rows, 0
        )
        chosen, factor = select_factor(candidates, node_pivots)
        results.append(solve_rows(chosen, factor, my_rows))
    root_rows = chosen.shape[0] // 2**LEVELS
    root_share = lax.dynamic_slice_in_dim(chosen, col_index % 2**LEVELS * root_rows, root_rows, 0)
    return (results[0], results[1], results[2], results[3], root_share)


def solution(mesh):
    finer = Mesh(mesh.devices.reshape(4, 4, 8, 2), ("row_0", "row_1", "col_0", "col_1"))
    placed = (
        P(None, ROW_COL),
        P(None, COL),
        P(None, COL),
        P(ROW_COL),
        P(ROW_COL, None),
        P(),
        P(),
        P(),
    )
    return jax.shard_map(
        body,
        mesh=finer,
        in_specs=placed,
        out_specs=(
            P(ROW_COL, None),
            P(ROW_COL, None),
            P(ROW_COL, None),
            P(ROW_COL, None),
            P(ROW_COL, None),
        ),
        check_vma=False,
    )
```

profile of v0, /device:TPU:1, one launch (start us, length us, event | category | flops | bytes accessed | tf_op | source)
XLA Modules:
  0.0 315.8 jit_solution(11301371426663765097)
XLA Ops:
  7.2 2.3 copy.50
  9.6 9.0 %all_to_all.10 = f32[4,2,512]{2,1,0:T(2,128)S(1)} all-to-all(f32[4,2,512]{2,1,0:T(2,128)S(1)} %broadcast_in_dim.51), channel_id=1, replica_groups=mesh['row_0'=4,'row_1'=4,'col_0'=8,'col_1'=2] {'row_0'}, dimensions={0} | all-to-all | bytes 32768 | tf_op jit(solution)/shard_map/all_to_all | solution.py:20
  19.8 13.6 %all-to-all-start.1 = ((f32[64,4,2,512]{3,1,2,0:T(4,128)}), f32[64,4,2,512]{3,1,2,0:T(4,128)S(1)}, u32[]{:S(2)}, u32[]{:S(2)}) async-start(f32[64,4,2,512]{3,1,2,0:T(4,128)} %broadcast_in_dim.52), calls=%async_computation.1 | async-start | bytes 2097152 | tf_op jit(solution)/shard_map/all_to_all | solution.py:20
  33.5 48.8 %all_gather.6 = bf16[2,32768]{1,0:T(2,128)(2,1)S(1)} all-gather(bf16[2,2048]{1,0:T(2,128)(2,1)S(1)} %copy-done), channel_id=1, replica_groups=mesh['row_0'=4,'row_1'=4,'col_0'=8,'col_1'=2] {'col_0','col_1'}, dimensions={1}, use_global_device_ids=true | all-gather | bytes 139264 | tf_op jit(solution)/shard_map/all_gather | solution.py:87
  84.6 30.6 %copy.61 = f32[64,4,2,512]{2,3,0,1:T(8,128)} copy(f32[64,4,2,512]{3,1,2,0:T(4,128)S(1)} %all-to-all-done.1) | data formatting | bytes 2097152 | tf_op jit(solution)/shard_map/transpose | solution.py:24
  115.2 3.6 %gather_fusion = f32[512,2]{1,0:T(8,128)S(1)} fusion(f32[2,131072]{0,1:T(8,128)} %bitcast.5, s32[1024]{0:T(1024)S(1)} %pad_clamp_fusion.4), kind=kCustom, calls=%fused_computation.3 | custom fusion | bytes 10240 | tf_op jit(solution)/shard_map/jit(_take)/gather | solution.py:83
  119.1 13.6 %all-gather.2.cloned.1.call-done = bf16[256,32768]{0,1:T(8,128)(2,1)} async-done(((bf16[256,2048]{0,1:T(8,128)(2,1)}), bf16[256,32768]{0,1:T(8,128)(2,1)}) %all-gather.2.cloned.1.call-update) | async-done | bytes 16777232 | tf_op jit(solution)/shard_map/all_gather | solution.py:88
  132.7 63.3 %while.11 = (s32[]{:T(128)}, f32[512,256]{1,0:T(8,128)S(1)}, f32[2,512]{1,0:T(2,128)S(1)}, bf16[32,2,1024]{2,1,0:T(2,128)(2,1)S(1)}, bf16[32,256,1024]{1,2,0:T(8,128)(2,1)}, /*index=5*/s32[]{:T(128)}, s32[]{:T(128)}, s32[]{}) while((s32[]{:T(128)}, f32[512,256]{1,0:T(8,128)S(1)}, f32[2,512]{1,0:T(2,128)S(1)}, ...), condition=%wide.region_1.2_spmd.clone, body=%wide.region_0.1_spmd.clone.sunk | while | flops 272893952 | bytes 1606259 | solution.py:98
  134.7 1.9 convolution_add_fusion.2
  136.7 1.9 convolution_add_fusion.2
  138.7 1.9 convolution_add_fusion.2
  160.4 1.9 convolution_add_fusion.2
  162.4 1.9 convolution_add_fusion.2
  164.4 1.9 convolution_add_fusion.2
  186.2 1.9 convolution_add_fusion.2
  199.8 11.7 %cholesky.74 = f32[128,128]{1,0:T(8,128)S(1)} custom-call(f32[128,128]{1,0:T(8,128)S(1)} %copy.54), custom_call_target="Cholesky" | custom-call | tf_op jit(solution)/shard_map/jit(cholesky)/cholesky | solution.py:58
  212.8 9.8 %custom-call.22 = f32[1,128,128]{1,2,0:T(8,128)S(1)} custom-call(f32[1,128,128]{2,1,0:T(8,128)S(1)} %fusion.13), custom_call_target="InvertDiagBlocksLowerTriangular" | custom-call | tf_op jit(solution)/shard_map/triangular_solve | solution.py:64
  227.4 11.7 %cholesky.85 = f32[128,128]{1,0:T(8,128)S(1)} custom-call(f32[128,128]{1,0:T(8,128)S(1)} %copy.56), custom_call_target="Cholesky" | custom-call | tf_op jit(solution)/shard_map/jit(cholesky)/cholesky | solution.py:58
  240.4 9.8 %custom-call.23 = f32[1,128,128]{1,2,0:T(8,128)S(1)} custom-call(f32[1,128,128]{2,1,0:T(8,128)S(1)} %fusion.14), custom_call_target="InvertDiagBlocksLowerTriangular" | custom-call | tf_op jit(solution)/shard_map/triangular_solve | solution.py:64
  252.6 3.0 collective-permute-start.2
  257.4 11.7 %cholesky.96 = f32[128,128]{1,0:T(8,128)S(1)} custom-call(f32[128,128]{1,0:T(8,128)S(1)} %copy.58), custom_call_target="Cholesky" | custom-call | tf_op jit(solution)/shard_map/jit(cholesky)/cholesky | solution.py:58
  270.4 9.8 %custom-call.24 = f32[1,128,128]{1,2,0:T(8,128)S(1)} custom-call(f32[1,128,128]{2,1,0:T(8,128)S(1)} %fusion.15), custom_call_target="InvertDiagBlocksLowerTriangular" | custom-call | tf_op jit(solution)/shard_map/triangular_solve | solution.py:64
  284.2 11.7 %cholesky.107 = f32[128,128]{1,0:T(8,128)S(1)} custom-call(f32[128,128]{1,0:T(8,128)S(1)} %copy.60), custom_call_target="Cholesky" | custom-call | tf_op jit(solution)/shard_map/jit(cholesky)/cholesky | solution.py:58
  297.3 9.8 %custom-call.25 = f32[1,128,128]{1,2,0:T(8,128)S(1)} custom-call(f32[1,128,128]{2,1,0:T(8,128)S(1)} %fusion.16), custom_call_target="InvertDiagBlocksLowerTriangular" | custom-call | tf_op jit(solution)/shard_map/triangular_solve | solution.py:64
  (179 shorter events, 73.2 us)
Async XLA Ops:
  7.2 2.4 copy-start.2
  7.2 125.5 %all-gather.2.cloned.1.call-start = ((), (), s32[]{:S(2)}) async-start(), calls=%async_computation.2 | async-start | bytes 17825792 | tf_op jit(solution)/shard_map/all_gather | solution.py:88
  9.5 24.0 %copy-start = (bf16[2,2048]{1,0:T(2,128)(2,1)S(1)}, bf16[2,2048]{1,0:T(2,128)(2,1)}, u32[]{:S(2)}) copy-start(bf16[2,2048]{1,0:T(2,128)(2,1)} %param.14) | copy-start | bytes 24580
  9.5 74.9 %copy-start.1 = (s32[512]{0:T(512)S(1)}, s32[512]{0:T(512)}, u32[]{:S(2)}) copy-start(s32[512]{0:T(512)} %param.16) | copy-start | bytes 6148
  9.5 74.9 %copy-start.3 = (s32[1,128]{1,0:T(1,128)S(1)}, s32[1,128]{1,0:T(1,128)}, u32[]{:S(2)}) copy-start(s32[1,128]{1,0:T(1,128)} %param.17) | copy-start | bytes 1540
  19.8 64.7 %all-to-all-start.1 = ((f32[64,4,2,512]{3,1,2,0:T(4,128)}), f32[64,4,2,512]{3,1,2,0:T(4,128)S(1)}, u32[]{:S(2)}, u32[]{:S(2)}) async-start(f32[64,4,2,512]{3,1,2,0:T(4,128)} %broadcast_in_dim.52), calls=%async_computation.1 | async-start | bytes 2097152 | tf_op jit(solution)/shard_map/all_to_all | solution.py:20
  196.9 27.5 %collective-permute-start = (f32[128,256]{1,0:T(8,128)S(1)}, f32[128,256]{1,0:T(8,128)S(1)}, u32[]{:S(2)}, u32[]{:S(2)}) collective-permute-start(f32[128,256]{1,0:T(8,128)S(1)} %broadcast_select_fusion.3), channel_id=1, source_target_pairs={{0,1},{1,0},{2,3},{3,2},{4,5},{5,4},{6,7},{7,6},{8,9},{9,8},{10,11... | collective-permute-start | bytes 393224 | tf_op jit(solution)/shard_map/ppermute | solution.py:42
  225.3 26.5 %collective-permute-start.1 = (f32[128,256]{1,0:T(8,128)S(1)}, f32[128,256]{1,0:T(8,128)S(1)}, u32[]{:S(2)}, u32[]{:S(2)}) collective-permute-start(f32[128,256]{1,0:T(8,128)S(1)} %broadcast_select_fusion.2), channel_id=1, source_target_pairs={{0,2},{2,0},{1,3},{3,1},{4,6},{6,4},{5,7},{7,5},{8,10},{10,8},{9,1... | collective-permute-start | bytes 393224 | tf_op jit(solution)/shard_map/ppermute | solution.py:42
  252.6 28.9 %collective-permute-start.2 = (f32[128,256]{1,0:T(8,128)S(1)}, f32[128,256]{1,0:T(8,128)S(1)}, u32[]{:S(2)}, u32[]{:S(2)}) collective-permute-start(f32[128,256]{1,0:T(8,128)S(1)} %broadcast_select_fusion.1), channel_id=1, source_target_pairs={{0,4},{4,0},{1,5},{5,1},{2,6},{6,2},{3,7},{7,3},{8,12},{12,8},{9,1... | collective-permute-start | bytes 393224 | tf_op jit(solution)/shard_map/ppermute | solution.py:42
Sparse Core Ops, SparseCore 0:
  9.8 122.7 all-gather.1
where the time goes:
time: 318 us; the launch traced here: 316 us
  other arithmetic  94.7 us (30%)
  matrix products  71.2 us (22%)
  blocking collectives  57.8 us (18%)
  local copies, waits for them, and re-layouts  42.5 us (13%)
  starting transfers between devices  17.4 us (5%)
  between operations  17.2 us (5%)
  waiting for transfers between devices  13.6 us (4%)
    dot_general x32, matrix products, sketch_product(): lax.dot_general(panel, weights, (((1,), (1,)), ((), ())), preferred_eleme...  61.3 us
    another operation x12, other arithmetic, select_factor(): return (chosen, jnp.linalg.cholesky(shifted))  49.6 us
    all_gather x1, blocking collectives, body(): lax.all_gather(sources, COL, axis=1, tiled=True)  48.8 us
    another operation x8, other arithmetic, solve_rows(): lax.linalg.triangular_solve(factor, first, left_side=True, lower=True, tr...  41.9 us
    transpose x1, local copies, waits for them, and re-layouts, laid_out(): parts = jnp.moveaxis(parts, 0, dim)  30.6 us
    all_to_all x1, starting transfers between devices, copy_for_each(): return lax.all_to_all(copies, axis, split_axis=0, concat_axis=0, tiled=True)  13.6 us
    all_gather x1, waiting for transfers between devices, body(): lax.all_gather(omega, COL, axis=1, tiled=True)  13.6 us
    all_to_all x1, blocking collectives, copy_for_each(): return lax.all_to_all(copies, axis, split_axis=0, concat_axis=0, tiled=True)  9.03 us
  transfers between devices with their start and end apart: 5, of which 1 were waited for; matrix products, arithmetic and copies ran while one was open for 36% of the time, Pallas kernels for 0%

commit v1 on v0

--- a/solution.py
+++ b/solution.py
@@ -85,7 +85,7 @@
     running = initial
     pieces = (
         lax.all_gather(sources, COL, axis=1, tiled=True),
-        lax.all_gather(omega, COL, axis=1, tiled=True),
+        jnp.concatenate(lax.all_to_all(jnp.stack([omega] * lax.axis_size(COL)), COL, 0, 0), axis=1),
     )
     width = pieces[0].shape[1]
     block_len = math.gcd(width, 1024)

time: 318 us -> 653 us (2.05)
  blocking collectives: 57.8 us -> 384 us
  waiting for transfers between devices: 13.6 us -> 27.1 us
  between operations: 17.2 us -> 3.77 us
    all_gather x1, blocking collectives: 48.8 us -> 375 us  [body(): lax.all_gather(sources, COL, axis=1, tiled=True)]
    all_to_all x1, waiting for transfers between devices: 0.01 us -> 27.1 us  [copy_for_each(): return lax.all_to_all(copies, axis, split_axis=0, concat_axis=0, tiled=True)]
    all_gather x1 -> x0, waiting for transfers between devices: 13.6 us -> none  [body(): lax.all_gather(omega, COL, axis=1, tiled=True)]
  transfers between devices with their start and end apart: 5 -> 5, of which waited for: 1 -> 1; matrix products, arithmetic and copies ran while one was open for 36% -> 18% of each run, Pallas kernels for 0% -> 0%
where the time goes in v1:
time: 653 us; the launch traced here: 651 us
  blocking collectives  384 us (59%)
  other arithmetic  94.7 us (15%)
  matrix products  71.1 us (11%)
  local copies, waits for them, and re-layouts  48 us (7%)
  waiting for transfers between devices  27.1 us (4%)
  starting transfers between devices  20.6 us (3%)
    all_gather x1, blocking collectives, body(): lax.all_gather(sources, COL, axis=1, tiled=True)  375 us
    dot_general x32, matrix products, sketch_product(): lax.dot_general(panel, weights, (((1,), (1,)), ((), ())), preferred_eleme...  61.3 us
    another operation x12, other arithmetic, select_factor(): return (chosen, jnp.linalg.cholesky(shifted))  49.6 us
    another operation x8, other arithmetic, solve_rows(): lax.linalg.triangular_solve(factor, first, left_side=True, lower=True, tr...  41.9 us
    transpose x1, local copies, waits for them, and re-layouts, laid_out(): parts = jnp.moveaxis(parts, 0, dim)  30.6 us
    all_to_all x1, waiting for transfers between devices, copy_for_each(): return lax.all_to_all(copies, axis, split_axis=0, concat_axis=0, tiled=True)  27.1 us
    all_to_all x1, starting transfers between devices, copy_for_each(): return lax.all_to_all(copies, axis, split_axis=0, concat_axis=0, tiled=True)  13.6 us
  transfers between devices with their start and end apart: 5, of which 1 were waited for; matrix products, arithmetic and copies ran while one was open for 18% of the time, Pallas kernels for 0%

profile of v1, /device:TPU:1, one launch (start us, length us, event | category | flops | bytes accessed | tf_op | source)
XLA Modules:
  0.0 650.8 jit_solution(18254533050767707236)
XLA Ops:
  1.3 9.0 %all_to_all.15 = f32[4,2,512]{2,1,0:T(2,128)S(1)} all-to-all(f32[4,2,512]{2,1,0:T(2,128)S(1)} %broadcast_in_dim.51), channel_id=1, replica_groups=mesh['row_0'=4,'row_1'=4,'col_0'=8,'col_1'=2] {'row_0'}, dimensions={0} | all-to-all | bytes 32768 | tf_op jit(solution)/shard_map/all_to_all | solution.py:20
  11.6 13.6 %all-to-all-start.1 = ((f32[64,4,2,512]{3,1,2,0:T(4,128)}), f32[64,4,2,512]{3,1,2,0:T(4,128)S(1)}, u32[]{:S(2)}, u32[]{:S(2)}) async-start(f32[64,4,2,512]{3,1,2,0:T(4,128)} %broadcast_in_dim.52), calls=%async_computation.1 | async-start | bytes 2097152 | tf_op jit(solution)/shard_map/all_to_all | solution.py:20
  26.7 27.1 %all-to-all-done.1 = f32[64,4,2,512]{3,1,2,0:T(4,128)S(1)} async-done(((f32[64,4,2,512]{3,1,2,0:T(4,128)}), f32[64,4,2,512]{3,1,2,0:T(4,128)S(1)}, u32[]{:S(2)}, u32[]{:S(2)}) %all-to-all-start.1) | async-done | bytes 1048608 | tf_op jit(solution)/shard_map/all_to_all | solution.py:20
  53.7 5.9 stack.2
  59.6 5.2 all-to-all-start.2
  64.9 375.0 %all_gather.3 = bf16[2,32768]{1,0:T(2,128)(2,1)S(1)} all-gather(bf16[2,2048]{1,0:T(2,128)(2,1)S(1)} %copy-done), channel_id=1, replica_groups=mesh['row_0'=4,'row_1'=4,'col_0'=8,'col_1'=2] {'col_0','col_1'}, dimensions={1}, use_global_device_ids=true | all-gather | bytes 139264 | tf_op jit(solution)/shard_map/all_gather | solution.py:87
  442.2 30.6 %copy.61 = f32[64,4,2,512]{2,3,0,1:T(8,128)} copy(f32[64,4,2,512]{3,1,2,0:T(4,128)S(1)} %all-to-all-done.1) | data formatting | bytes 2097152 | tf_op jit(solution)/shard_map/transpose | solution.py:24
  472.8 3.5 gather_fusion
  476.6 63.3 %while.11 = (s32[]{:T(128)}, f32[512,256]{1,0:T(8,128)S(1)}, f32[2,512]{1,0:T(2,128)S(1)}, bf16[32,2,1024]{2,1,0:T(2,128)(2,1)S(1)}, bf16[32,256,1024]{1,2,0:T(8,128)(2,1)}, /*index=5*/s32[]{:T(128)}, s32[]{:T(128)}, s32[]{}) while((s32[]{:T(128)}, f32[512,256]{1,0:T(8,128)S(1)}, f32[2,512]{1,0:T(2,128)S(1)}, ...), condition=%wide.region_1.2_spmd.clone, body=%wide.region_0.1_spmd.clone.sunk | while | flops 272893952 | bytes 1606259 | solution.py:98
  476.6 1.9 convolution_add_fusion.2
  496.4 1.9 convolution_add_fusion.2
  498.4 1.9 convolution_add_fusion.2
  500.4 1.9 convolution_add_fusion.2
  522.1 1.9 convolution_add_fusion.2
  524.1 1.9 convolution_add_fusion.2
  526.1 1.9 convolution_add_fusion.2
  543.6 11.7 %cholesky.74 = f32[128,128]{1,0:T(8,128)S(1)} custom-call(f32[128,128]{1,0:T(8,128)S(1)} %copy.54), custom_call_target="Cholesky" | custom-call | tf_op jit(solution)/shard_map/jit(cholesky)/cholesky | solution.py:58
  556.7 9.8 %custom-call.22 = f32[1,128,128]{1,2,0:T(8,128)S(1)} custom-call(f32[1,128,128]{2,1,0:T(8,128)S(1)} %fusion.13), custom_call_target="InvertDiagBlocksLowerTriangular" | custom-call | tf_op jit(solution)/shard_map/triangular_solve | solution.py:64
  571.2 11.7 %cholesky.85 = f32[128,128]{1,0:T(8,128)S(1)} custom-call(f32[128,128]{1,0:T(8,128)S(1)} %copy.56), custom_call_target="Cholesky" | custom-call | tf_op jit(solution)/shard_map/jit(cholesky)/cholesky | solution.py:58
  584.2 9.8 %custom-call.23 = f32[1,128,128]{1,2,0:T(8,128)S(1)} custom-call(f32[1,128,128]{2,1,0:T(8,128)S(1)} %fusion.14), custom_call_target="InvertDiagBlocksLowerTriangular" | custom-call | tf_op jit(solution)/shard_map/triangular_solve | solution.py:64
  599.2 11.7 %cholesky.96 = f32[128,128]{1,0:T(8,128)S(1)} custom-call(f32[128,128]{1,0:T(8,128)S(1)} %copy.58), custom_call_target="Cholesky" | custom-call | tf_op jit(solution)/shard_map/jit(cholesky)/cholesky | solution.py:58
  612.3 9.8 %custom-call.24 = f32[1,128,128]{1,2,0:T(8,128)S(1)} custom-call(f32[1,128,128]{2,1,0:T(8,128)S(1)} %fusion.15), custom_call_target="InvertDiagBlocksLowerTriangular" | custom-call | tf_op jit(solution)/shard_map/triangular_solve | solution.py:64
  626.1 11.7 %cholesky.107 = f32[128,128]{1,0:T(8,128)S(1)} custom-call(f32[128,128]{1,0:T(8,128)S(1)} %copy.60), custom_call_target="Cholesky" | custom-call | tf_op jit(solution)/shard_map/jit(cholesky)/cholesky | solution.py:58
  639.1 9.8 %custom-call.25 = f32[1,128,128]{1,2,0:T(8,128)S(1)} custom-call(f32[1,128,128]{2,1,0:T(8,128)S(1)} %fusion.16), custom_call_target="InvertDiagBlocksLowerTriangular" | custom-call | tf_op jit(solution)/shard_map/triangular_solve | solution.py:64
  (177 shorter events, 76.3 us)
Async XLA Ops:
  11.6 42.1 %all-to-all-start.1 = ((f32[64,4,2,512]{3,1,2,0:T(4,128)}), f32[64,4,2,512]{3,1,2,0:T(4,128)S(1)}, u32[]{:S(2)}, u32[]{:S(2)}) async-start(f32[64,4,2,512]{3,1,2,0:T(4,128)} %broadcast_in_dim.52), calls=%async_computation.1 | async-start | bytes 2097152 | tf_op jit(solution)/shard_map/all_to_all | solution.py:20
  59.6 5.3 copy-start
  59.6 382.5 %copy-start.1 = (s32[512]{0:T(512)S(1)}, s32[512]{0:T(512)}, u32[]{:S(2)}) copy-start(s32[512]{0:T(512)} %param.16) | copy-start | bytes 6148
  59.6 382.5 %copy-start.2 = (s32[1,128]{1,0:T(1,128)S(1)}, s32[1,128]{1,0:T(1,128)}, u32[]{:S(2)}) copy-start(s32[1,128]{1,0:T(1,128)} %param.17) | copy-start | bytes 1540
  59.6 416.9 %all-to-all-start.2 = ((bf16[16,256,2048]{1,2,0:T(8,128)(2,1)}), bf16[16,256,2048]{1,2,0:T(8,128)(2,1)}, u32[]{:S(2)}, u32[]{:S(2)}) async-start(bf16[16,256,2048]{1,2,0:T(8,128)(2,1)} %stack.2), calls=%async_computation.2 | async-start | bytes 33554432 | tf_op jit(solution)/shard_map/all_to_all | solution.py:88
  540.8 27.4 %collective-permute-start = (f32[128,256]{1,0:T(8,128)S(1)}, f32[128,256]{1,0:T(8,128)S(1)}, u32[]{:S(2)}, u32[]{:S(2)}) collective-permute-start(f32[128,256]{1,0:T(8,128)S(1)} %broadcast_select_fusion.3), channel_id=1, source_target_pairs={{0,1},{1,0},{2,3},{3,2},{4,5},{5,4},{6,7},{7,6},{8,9},{9,8},{10,11... | collective-permute-start | bytes 393224 | tf_op jit(solution)/shard_map/ppermute | solution.py:42
  569.1 26.5 %collective-permute-start.1 = (f32[128,256]{1,0:T(8,128)S(1)}, f32[128,256]{1,0:T(8,128)S(1)}, u32[]{:S(2)}, u32[]{:S(2)}) collective-permute-start(f32[128,256]{1,0:T(8,128)S(1)} %broadcast_select_fusion.2), channel_id=1, source_target_pairs={{0,2},{2,0},{1,3},{3,1},{4,6},{6,4},{5,7},{7,5},{8,10},{10,8},{9,1... | collective-permute-start | bytes 393224 | tf_op jit(solution)/shard_map/ppermute | solution.py:42
  596.4 27.0 %collective-permute-start.2 = (f32[128,256]{1,0:T(8,128)S(1)}, f32[128,256]{1,0:T(8,128)S(1)}, u32[]{:S(2)}, u32[]{:S(2)}) collective-permute-start(f32[128,256]{1,0:T(8,128)S(1)} %broadcast_select_fusion.1), channel_id=1, source_target_pairs={{0,4},{4,0},{1,5},{5,1},{2,6},{6,2},{3,7},{7,3},{8,12},{12,8},{9,1... | collective-permute-start | bytes 393224 | tf_op jit(solution)/shard_map/ppermute | solution.py:42
